TPU v7x, 32 devices: a whole 2x2x4 slice. The times are simulated.
32 devices in a mesh: seq: 8 (over z, y), head: 4 (over x, core).
Axes of the slice: x: 2, y: 2, z: 4, core: 2. Of those that a mesh axis runs over, the one named last changes fastest.
Arguments:
- tokens: bfloat16 [1024, 1024], P('seq'), may hold values from -6 to 6
- cotangent: bfloat16 [1024, 1024], P('seq'), may hold values from -6 to 6
- gate_code: int32 [2, 1024, 8], P(None, 'seq', 'head'), may hold values from 0 to 723000
- beta_code: int32 [2, 1024, 8], P(None, 'seq', 'head'), may hold values from 256 to 1024
- norm1_gain: float32 [2, 1024], replicated, may hold values from 0.5 to 1.5
- weight_in: bfloat16 [2, 1024, 6144], P(None, None, 'head'), may hold values from -0.1875 to 0.1875
- conv_weight: bfloat16 [2, 4, 4096], P(None, None, 'head'), may hold values from -3 to 3
- out_gain: float32 [2, 256], replicated, may hold values from 0.5 to 1.5
- weight_out: bfloat16 [2, 2048, 1024], P(None, 'head'), may hold values from -0.25 to 0.25
- norm2_gain: float32 [2, 1024], replicated, may hold values from 0.5 to 1.5
- weight_gate: bfloat16 [2, 1024, 2816], P(None, None, 'head'), may hold values from -0.1875 to 0.1875
- weight_up: bfloat16 [2, 1024, 2816], P(None, None, 'head'), may hold values from -0.1875 to 0.1875
- weight_down: bfloat16 [2, 2816, 1024], P(None, 'head'), may hold values from -0.21875 to 0.21875
Outputs:
- activations: bfloat16 [1024, 1024], P('seq')
- input_grad: float32 [1024, 1024], P('seq')
- grad_norm1_gain: float32 [2, 1024], replicated
- grad_weight_in: float32 [2, 1024, 6144], P(None, 'seq', 'head')
- grad_conv_weight: float32 [2, 4, 4096], P(None, None, 'head')
- grad_out_gain: float32 [2, 256], replicated
- grad_weight_out: float32 [2, 2048, 1024], P(None, 'head', 'seq')
- grad_norm2_gain: float32 [2, 1024], replicated
- grad_weight_gate: float32 [2, 1024, 2816], P(None, 'seq', 'head')
- grad_weight_up: float32 [2, 1024, 2816], P(None, 'seq', 'head')
- grad_weight_down: float32 [2, 2816, 1024], P(None, 'head', 'seq')
All inputs are finite; a program needn't handle non-finite values.
Results may differ from a plain program's by a relative error of at most 0.02.
Values sent between devices are 32-bit elements; how exact they have to be, the bound alone decides.
No kernel may reach another device: no remote copies, remote signals or barrier semaphores. Data moves between devices by JAX's collectives and lax.ppermute only.
A program may use at most 256 MiB of HBM per device.

v0:
```python
import jax
import jax.numpy as jnp
from jax import lax
from jax.sharding import PartitionSpec as P

DK = 128
DV = 256
CONV = 4
SPAN = 64
STACK_LEVELS = 2
highest = lax.Precision.HIGHEST
norm_eps = 1e-06
gate_unit = 1.0 / 1048576.0
beta_unit = 1.0 / 1024.0


def from_behind(array, axis, by):
    length = lax.axis_size(axis)
    pairs = [(i, i + by) for i in range(length) if 0 <= i + by < length]
    return lax.ppermute(array, axis, pairs)


def rms_norm(stream, gain):
    return stream * lax.rsqrt(jnp.mean(stream * stream, axis=-1, keepdims=True) + norm_eps) * gain


def unit_rows(vectors):
    return vectors * lax.rsqrt(jnp.sum(vectors * vectors, axis=-1, keepdims=True) + norm_eps)


def swiglu(gate_pre, up_pre):
    return jax.nn.silu(gate_pre) * up_pre


def post_mix(outputs, gate_z, gain):
    return rms_norm(outputs, gain) * jax.nn.silu(gate_z)


def mixer_inputs(windowed, conv_taps):
    length_total = windowed.shape[0] - (CONV - 1)
    conv_out = conv_taps[0] * windowed[CONV - 1 :]
    for tap_index in range(1, CONV):
        conv_out = (
            conv_out
            + conv_taps[tap_index]
            * windowed[CONV - 1 - tap_index : CONV - 1 - tap_index + length_total]
        )
    active = jax.nn.silu(conv_out).reshape(length_total, -1, 2 * DK + DV)
    queries = unit_rows(active[:, :, :DK]) * DK ** (-0.5)
    keys_unit = unit_rows(active[:, :, DK : 2 * DK])
    return (queries, keys_unit, active[:, :, 2 * DK :])


def span_step(carry_state, pieces):
    queries, keys_unit, values_in, logdecay, beta_rate = pieces
    block_len = queries.shape[0]
    cumulated = jnp.cumsum(logdecay, axis=0)
    cum_heads = jnp.transpose(cumulated)
    row_index = lax.broadcasted_iota(jnp.int32, (1, block_len, block_len), 1)
    col_index = lax.broadcasted_iota(jnp.int32, (1, block_len, block_len), 2)
    inclusive = row_index >= col_index
    log_ratio = jnp.where(inclusive, cum_heads[:, :, None] - cum_heads[:, None, :], 0.0)
    decay_ratio = jnp.where(inclusive, jnp.exp(log_ratio), 0.0)
    beta_heads = jnp.transpose(beta_rate)
    key_key = jnp.einsum("thd,shd->hts", keys_unit, keys_unit, precision=highest)
    strict_lower = jnp.where(
        row_index > col_index, beta_heads[:, :, None] * decay_ratio * key_key, 0.0
    )
    system = strict_lower + jnp.eye(block_len, dtype=strict_lower.dtype)[None]
    decay_all = jnp.exp(cumulated)
    right_side = jnp.concatenate(
        [beta_rate[:, :, None] * values_in, (beta_rate * decay_all)[:, :, None] * keys_unit], axis=2
    )
    right_side = jnp.transpose(right_side, (1, 0, 2))
    solved_system = lax.linalg.triangular_solve(system, right_side, left_side=True, lower=True)
    val_width = values_in.shape[2]
    new_values = solved_system[:, :, :val_width] - jnp.einsum(
        "htd,hvd->htv", solved_system[:, :, val_width:], carry_state, precision=highest
    )
    query_key = jnp.einsum("thd,shd->hts", queries, keys_unit, precision=highest)
    mixing = decay_ratio * query_key
    outputs = jnp.transpose(decay_all)[:, :, None] * jnp.einsum(
        "thd,hvd->htv", queries, carry_state, precision=highest
    )
    outputs = outputs + jnp.einsum("hts,hsv->htv", mixing, new_values, precision=highest)
    to_end = jnp.exp(cumulated[-1][None, :] - cumulated)
    new_state = jnp.exp(cumulated[-1])[:, None, None] * carry_state
    new_state = new_state + jnp.einsum(
        "hsv,shd->hvd", new_values, to_end[:, :, None] * keys_unit, precision=highest
    )
    return (new_state, jnp.transpose(outputs, (1, 0, 2)))


def delta_rule(queries, keys_unit, values_in, logdecay, beta_rate, carry_state):
    length_total = queries.shape[0]
    block_count = length_total // SPAN

    def blocks(tensor):
        return tensor.reshape((block_count, SPAN) + tensor.shape[1:])

    final_state, outputs = lax.scan(
        span_step,
        carry_state,
        (
            blocks(queries),
            blocks(keys_unit),
            blocks(values_in),
            blocks(logdecay),
            blocks(beta_rate),
        ),
    )
    return (outputs.reshape((length_total,) + outputs.shape[2:]), final_state)


def state_prefix(transfer, offset):
    all_transfer, all_offset = (
        lax.all_gather(transfer, "seq", axis=0, tiled=True),
        lax.all_gather(offset, "seq", axis=0, tiled=True),
    )
    devices = lax.axis_size("seq")
    position = lax.axis_index("seq")
    transfer_kept = all_transfer.reshape((devices,) + transfer.shape)
    offsets_all = all_offset.reshape((devices,) + offset.shape)

    def advance(index_now, carry_state):
        moved = (
            jnp.einsum("hvj,hjk->hvk", carry_state, transfer_kept[index_now], precision=highest)
            + offsets_all[index_now]
        )
        return jnp.where(index_now < position, moved, carry_state)

    incoming = lax.fori_loop(0, devices, advance, jnp.zeros_like(offset))
    return (incoming, transfer_kept)


def state_back(transfer_kept, local_grad):
    all_grad = lax.all_gather(local_grad, "seq", axis=0, tiled=True)
    devices = lax.axis_size("seq")
    position = lax.axis_index("seq")
    grads_all = all_grad.reshape((devices,) + local_grad.shape)

    def retreat(step_index, carry_state):
        index_now = devices - 1 - step_index
        moved = (
            jnp.einsum("hvj,hkj->hvk", carry_state, transfer_kept[index_now], precision=highest)
            + grads_all[index_now]
        )
        return jnp.where(index_now > position, moved, carry_state)

    outgoing = lax.fori_loop(0, devices, retreat, jnp.zeros_like(local_grad))
    return outgoing


def head_total(partial_sum):
    share = lax.psum_scatter(partial_sum, "head", scatter_dimension=1, tiled=True)
    return lax.all_gather(share, "head", axis=1, tiled=True)


def layer_forward(stream, logdecay, beta_rate, weights):
    (
        gain_one,
        weight_in,
        conv_weight,
        out_gain,
        weight_out,
        gain_two,
        weight_gate,
        weight_up,
        weight_down,
    ) = weights
    length_total = stream.shape[0]
    normed = rms_norm(stream, gain_one).astype(jnp.bfloat16)
    projected = jnp.dot(normed, weight_in, preferred_element_type=jnp.float32).reshape(
        length_total, -1, 2 * DK + 2 * DV
    )
    head_count = projected.shape[1]
    conv_input = projected[:, :, : 2 * DK + DV].reshape(length_total, -1)
    gate_z = projected[:, :, 2 * DK + DV :]
    before = from_behind(conv_input[length_total - (CONV - 1) :], "seq", 1)
    windowed = jnp.concatenate([before, conv_input], axis=0)
    conv_taps = conv_weight.astype(jnp.float32)
    queries, keys_unit, values_in = mixer_inputs(windowed, conv_taps)
    wide_values = jnp.concatenate(
        [values_in, jnp.zeros((length_total, head_count, DK), jnp.float32)], axis=2
    )
    start_state = jnp.concatenate(
        [
            jnp.zeros((head_count, DV, DK), jnp.float32),
            jnp.broadcast_to(jnp.eye(DK, dtype=jnp.float32), (head_count, DK, DK)),
        ],
        axis=1,
    )
    wide_out, wide_end = delta_rule(
        queries, keys_unit, wide_values, logdecay, beta_rate, start_state
    )
    carried = wide_out[:, :, DV:]
    incoming, transfer_kept = state_prefix(wide_end[:, DV:], wide_end[:, :DV])
    outputs = wide_out[:, :, :DV] + jnp.einsum("thd,hvd->thv", carried, incoming, precision=highest)
    gated_out = post_mix(outputs, gate_z, out_gain).reshape(length_total, -1).astype(jnp.bfloat16)
    stream_mid = stream + head_total(
        jnp.dot(gated_out, weight_out, preferred_element_type=jnp.float32)
    )
    second_normed = rms_norm(stream_mid, gain_two).astype(jnp.bfloat16)
    gate_pre = jnp.dot(second_normed, weight_gate, preferred_element_type=jnp.float32)
    up_pre = jnp.dot(second_normed, weight_up, preferred_element_type=jnp.float32)
    hidden = swiglu(gate_pre, up_pre).astype(jnp.bfloat16)
    stream_next = stream_mid + head_total(
        jnp.dot(hidden, weight_down, preferred_element_type=jnp.float32)
    )
    stored = (
        stream,
        normed,
        windowed,
        conv_taps,
        gate_z,
        queries,
        keys_unit,
        values_in,
        outputs,
        carried,
        incoming,
        transfer_kept,
        gated_out,
        stream_mid,
        second_normed,
        gate_pre,
        up_pre,
        hidden,
    )
    return (stream_next, stored)


def layer_backward(grad_stream, logdecay, beta_rate, weights, stored):
    (
        gain_one,
        weight_in,
        conv_weight,
        out_gain,
        weight_out,
        gain_two,
        weight_gate,
        weight_up,
        weight_down,
    ) = weights
    (
        stream,
        normed,
        windowed,
        conv_taps,
        gate_z,
        queries,
        keys_unit,
        values_in,
        outputs,
        carried,
        incoming,
        transfer_kept,
        gated_out,
        stream_mid,
        second_normed,
        gate_pre,
        up_pre,
        hidden,
    ) = stored
    length_total = grad_stream.shape[0]
    back_bf = grad_stream.astype(jnp.bfloat16)
    grad_down = jnp.dot(hidden.T, back_bf, preferred_element_type=jnp.float32)
    grad_hidden = jnp.dot(back_bf, weight_down.T, preferred_element_type=jnp.float32)
    _, act_pull = jax.vjp(swiglu, gate_pre, up_pre)
    grad_gate_pre, grad_up_pre = act_pull(grad_hidden)
    grad_gate_pre = grad_gate_pre.astype(jnp.bfloat16)
    grad_up_pre = grad_up_pre.astype(jnp.bfloat16)
    grad_gate = jnp.dot(second_normed.T, grad_gate_pre, preferred_element_type=jnp.float32)
    grad_up = jnp.dot(second_normed.T, grad_up_pre, preferred_element_type=jnp.float32)
    ffn_partial = jnp.dot(
        grad_gate_pre, weight_gate.T, preferred_element_type=jnp.float32
    ) + jnp.dot(grad_up_pre, weight_up.T, preferred_element_type=jnp.float32)
    grad_normed_two = lax.psum(ffn_partial, "head")
    _, norm_pull = jax.vjp(rms_norm, stream_mid, gain_two)
    grad_mid, grad_gain_two = norm_pull(grad_normed_two)
    grad_stream = grad_stream + grad_mid
    back_bf = grad_stream.astype(jnp.bfloat16)
    grad_out = jnp.dot(gated_out.T, back_bf, preferred_element_type=jnp.float32)
    grad_gated = jnp.dot(back_bf, weight_out.T, preferred_element_type=jnp.float32).reshape(
        length_total, -1, DV
    )
    _, post_pull = jax.vjp(post_mix, outputs, gate_z, out_gain)
    grad_outputs, grad_gate_z, gain_mid_part = post_pull(grad_gated)
    local_grad = jnp.einsum("thv,thd->hvd", grad_outputs, carried, precision=highest)
    outgoing = state_back(transfer_kept, local_grad)

    def core_rule(queries, keys_unit, values_in):
        return delta_rule(queries, keys_unit, values_in, logdecay, beta_rate, incoming)

    _, rule_pull = jax.vjp(core_rule, queries, keys_unit, values_in)
    grad_queries, grad_keys, grad_values = rule_pull((grad_outputs, outgoing))
    _, mix_pull = jax.vjp(mixer_inputs, windowed, conv_taps)
    grad_window, grad_conv = mix_pull((grad_queries, grad_keys, grad_values))
    from_next = from_behind(grad_window[: CONV - 1], "seq", -1)
    grad_conv_in = grad_window[CONV - 1 :] + jnp.pad(
        from_next, ((length_total - (CONV - 1), 0), (0, 0))
    )
    grad_proj = (
        jnp.concatenate([grad_conv_in.reshape(length_total, -1, 2 * DK + DV), grad_gate_z], axis=2)
        .reshape(length_total, -1)
        .astype(jnp.bfloat16)
    )
    grad_in = jnp.dot(normed.T, grad_proj, preferred_element_type=jnp.float32)
    mixer_partial = jnp.dot(grad_proj, weight_in.T, preferred_element_type=jnp.float32)
    grad_normed, grad_out_gain = lax.psum((mixer_partial, gain_mid_part), "head")
    _, norm_pull = jax.vjp(rms_norm, stream, gain_one)
    grad_prev, grad_gain_one = norm_pull(grad_normed)
    return (
        grad_stream + grad_prev,
        (
            grad_gain_one,
            grad_in,
            grad_conv,
            grad_out_gain,
            grad_out,
            grad_gain_two,
            grad_gate,
            grad_up,
            grad_down,
        ),
    )


def body(
    tokens,
    cotangent,
    gate_code,
    beta_code,
    norm1_gain,
    weight_in,
    conv_weight,
    out_gain,
    weight_out,
    norm2_gain,
    weight_gate,
    weight_up,
    weight_down,
):
    logdecay = -gate_code.astype(jnp.float32) * gate_unit
    beta_rate = beta_code.astype(jnp.float32) * beta_unit
    everything = (
        norm1_gain,
        weight_in,
        conv_weight,
        out_gain,
        weight_out,
        norm2_gain,
        weight_gate,
        weight_up,
        weight_down,
    )
    stream = tokens.astype(jnp.float32)
    kept_layers = []
    for layer_idx in range(STACK_LEVELS):
        weights = tuple((tensor[layer_idx] for tensor in everything))
        stream, stored = layer_forward(stream, logdecay[layer_idx], beta_rate[layer_idx], weights)
        kept_layers.append((weights, stored))
    activations = stream.astype(jnp.bfloat16)
    grad_stream = cotangent.astype(jnp.float32)
    large_grads = []
    small_grads = []
    for layer_idx in reversed(range(STACK_LEVELS)):
        weights, stored = kept_layers[layer_idx]
        grad_stream, layer_part = layer_backward(
            grad_stream, logdecay[layer_idx], beta_rate[layer_idx], weights, stored
        )
        large_part = (layer_part[1], layer_part[4], layer_part[6], layer_part[7], layer_part[8])
        large_grads.insert(0, large_part)
        small_grads.insert(0, (layer_part[2], layer_part[0], layer_part[3], layer_part[5]))
    large_stack = tuple(
        (
            jnp.stack([grad_group[slot_index] for grad_group in large_grads])
            for slot_index in range(5)
        )
    )
    large_stack = (
        lax.psum_scatter(large_stack[0], "seq", scatter_dimension=1, tiled=True),
        lax.psum_scatter(large_stack[1], "seq", scatter_dimension=2, tiled=True),
        lax.psum_scatter(large_stack[2], "seq", scatter_dimension=1, tiled=True),
        lax.psum_scatter(large_stack[3], "seq", scatter_dimension=1, tiled=True),
        lax.psum_scatter(large_stack[4], "seq", scatter_dimension=2, tiled=True),
    )
    small_stack = tuple(
        (
            jnp.stack([grad_group[slot_index] for grad_group in small_grads])
            for slot_index in range(4)
        )
    )
    conv_grad, gain_one_grad, out_gain_grad, gain_two_grad = lax.psum(
        (small_stack[0], small_stack[1], small_stack[2], small_stack[3]), "seq"
    )
    return (
        activations,
        grad_stream,
        gain_one_grad,
        large_stack[0],
        conv_grad,
        out_gain_grad,
        large_stack[1],
        gain_two_grad,
        large_stack[2],
        large_stack[3],
        large_stack[4],
    )


def solution(mesh):
    in_specs = (
        P("seq", None),
        P("seq", None),
        P(None, "seq", "head"),
        P(None, "seq", "head"),
        P(),
        P(None, None, "head"),
        P(None, None, "head"),
        P(),
        P(None, "head", None),
        P(),
        P(None, None, "head"),
        P(None, None, "head"),
        P(None, "head", None),
    )
    out_specs = (
        P("seq", None),
        P("seq", None),
        P(),
        P(None, "seq", "head"),
        P(None, None, "head"),
        P(),
        P(None, "head", "seq"),
        P(),
        P(None, "seq", "head"),
        P(None, "seq", "head"),
        P(None, "head", "seq"),
    )
    return jax.shard_map(body, mesh=mesh, in_specs=in_specs, out_specs=out_specs, check_vma=False)
```

profile of v0, /device:TPU:0, one launch (start us, length us, event | category | flops | bytes accessed | tf_op | source)
XLA Modules:
  0.0 1594.9 jit_solution(10691709195272504350)
XLA Ops:
  26.3 10.4 collective-permute-done
  41.2 28.4 %while.210 = (s32[]{:T(128)}, f32[2,384,128]{2,1,0:T(8,128)S(1)}, f32[2,64,2,384]{3,1,0,2:T(8,128)S(1)}, f32[2,64,2]{1,2,0:T(2,128)S(1)}, f32[2,64,2]{1,2,0:T(2,...) while((s32[]{:T(128)}, f32[2,384,128]{2,1,0:T(8,128)S(1)}, ...), condition=%wide.region_5.7_spmd, body=%wide.region_3.6_spmd.sunk | while | flops 340353152 | bytes 4627117 | solution.py:101
  71.3 41.7 %all-gather.7.cloned.1.call-done = f32[16,128,128]{2,1,0:T(8,128)} async-done(((f32[2,128,128]{2,1,0:T(8,128)}), f32[16,128,128]{2,1,0:T(8,128)}) %all-gather.7.cloned.1.call-update) | async-done | bytes 1048592 | tf_op jit(solution)/shard_map/all_gather | solution.py:117
  113.0 50.5 %all-gather.9.cloned.1.call-done = f32[16,256,128]{2,1,0:T(8,128)} async-done(((f32[2,256,128]{2,1,0:T(8,128)}), f32[16,256,128]{2,1,0:T(8,128)}) %all-gather.9.cloned.1.call-update) | async-done | bytes 2097168 | tf_op jit(solution)/shard_map/all_gather | solution.py:118
  163.5 20.1 %while.216 = (s32[]{:T(128)}, f32[2,256,128]{1,2,0:T(8,128)S(1)}, s32[]{:T(128)}, f32[8,2,128,128]{3,2,1,0:T(8,128)}, f32[8,2,256,128]{3,2,1,0:T(8,128)}, /*index=5*/s32[]{:T(128)}, s32[]{:T(128)}) while((s32[]{:T(128)}, f32[2,256,128]{1,2,0:T(8,128)S(1)}, s32[]{:T(128)}, f32[8,2,128,128]{3,2,1,0:T(8,128)}, ...), condition=%wide.region_7.9_spmd.clone, body=%wide.region_6.8_spmd.clone.sunk | while | flops 100925440 | bytes 2754667 | solution.py:132
  187.0 20.2 %reduce-scatter.10.cloned.1.call-done = f32[128,256]{1,0:T(8,128)} async-done(((f32[128,1024]{1,0:T(8,128)}), f32[128,256]{1,0:T(8,128)}) %reduce-scatter.10.cloned.1.call-update) | async-done | bytes 131088 | tf_op jit(solution)/shard_map/reduce_scatter | solution.py:155
  223.9 17.5 %reduce-scatter.12.cloned.1.call-done = f32[128,256]{1,0:T(8,128)} async-done(((f32[128,1024]{1,0:T(8,128)}), f32[128,256]{1,0:T(8,128)}) %reduce-scatter.12.cloned.1.call-update) | async-done | bytes 131088 | tf_op jit(solution)/shard_map/reduce_scatter | solution.py:155
  275.9 30.3 %while.211 = (s32[]{:T(128)}, f32[2,384,128]{2,1,0:T(8,128)S(1)}, f32[2,64,2,384]{3,1,0,2:T(8,128)S(1)}, f32[2,64,2]{1,2,0:T(2,128)S(1)}, f32[2,64,2]{1,2,0:T(2,...) while((s32[]{:T(128)}, f32[2,384,128]{2,1,0:T(8,128)S(1)}, ...), condition=%wide.region_17.19_spmd, body=%wide.region_15.18_spmd.sunk | while | flops 340353152 | bytes 4627117 | solution.py:101
  307.8 41.1 %all-gather.11.cloned.1.call-done = f32[16,128,128]{2,1,0:T(8,128)} async-done(((f32[2,128,128]{2,1,0:T(8,128)}), f32[16,128,128]{2,1,0:T(8,128)}) %all-gather.11.cloned.1.call-update) | async-done | bytes 1048592 | tf_op jit(solution)/shard_map/all_gather | solution.py:117
  348.9 50.4 %all-gather.13.cloned.1.call-done = f32[16,256,128]{2,1,0:T(8,128)} async-done(((f32[2,256,128]{2,1,0:T(8,128)}), f32[16,256,128]{2,1,0:T(8,128)}) %all-gather.13.cloned.1.call-update) | async-done | bytes 2097168 | tf_op jit(solution)/shard_map/all_gather | solution.py:118
  399.3 20.0 %while.217 = (s32[]{:T(128)}, f32[2,256,128]{1,2,0:T(8,128)S(1)}, s32[]{:T(128)}, f32[8,2,128,128]{3,2,1,0:T(8,128)}, f32[8,2,256,128]{3,2,1,0:T(8,128)}, /*index=5*/s32[]{:T(128)}, s32[]{:T(128)}) while((s32[]{:T(128)}, f32[2,256,128]{1,2,0:T(8,128)S(1)}, s32[]{:T(128)}, f32[8,2,128,128]{3,2,1,0:T(8,128)}, ...), condition=%wide.region_19.21_spmd.clone, body=%wide.region_18.20_spmd.clone.sunk | while | flops 100925440 | bytes 2754667 | solution.py:132
  426.3 17.6 %reduce-scatter.14.cloned.1.call-done = f32[128,256]{1,0:T(8,128)} async-done(((f32[128,1024]{1,0:T(8,128)}), f32[128,256]{1,0:T(8,128)}) %reduce-scatter.14.cloned.1.call-update) | async-done | bytes 131088 | tf_op jit(solution)/shard_map/reduce_scatter | solution.py:155
  462.5 28.1 %all-reduce.38.cloned.1.call-done = f32[128,1024]{1,0:T(8,128)} async-done(((f32[128,1024]{1,0:T(8,128)}), f32[128,1024]{1,0:T(8,128)}) %all-reduce.38.cloned.1.call-update) | async-done | bytes 524304 | tf_op jit(solution)/shard_map/psum | solution.py:278
  492.4 23.1 %reduce-scatter.16.cloned.1.call-done = f32[128,256]{1,0:T(8,128)} async-done(((f32[128,1024]{1,0:T(8,128)}), f32[128,256]{1,0:T(8,128)}) %reduce-scatter.16.cloned.1.call-update) | async-done | bytes 131088 | tf_op jit(solution)/shard_map/reduce_scatter | solution.py:155
  535.7 39.1 %while.214 = (s32[]{:T(128)}, f32[2,256,128]{2,1,0:T(8,128)S(1)}, f32[2,2,64,64]{3,2,1,0:T(8,128)}, f32[2,64,2,1]{1,2,3,0:T(2,128)S(1)}, f32[2,64,2,1]{1,2,3,0:T...) while((s32[]{:T(128)}, f32[2,256,128]{2,1,0:T(8,128)S(1)}, ...), condition=%wide.region_31.34_spmd.clone.clone, body=%wide.region_29.33_spmd.clone.clone.sunk | while | flops 164024704 | bytes 3933053 | solution.py:101
  541.2 9.9 custom-call.38
  579.9 32.3 %while.218 = (s32[]{:T(128)}, f32[2,256,128]{1,2,0:T(8,128)}, s32[]{:T(128)}, f32[8,2,128,128]{3,2,1,0:T(8,128)}, f32[8,2,256,128]{3,2,1,0:T(8,128)}, /*index=5*/s32[]{:T(128)}, s32[]{:T(128)}, s32[]{:T(128)}, s32[]{:T(128)}) while((s32[]{:T(128)}, f32[2,256,128]{1,2,0:T(8,128)}, s32[]{:T(128)}, f32[8,2,128,128]{3,2,1,0:T(8,128)}, ...), condition=%wide.region_28.30_spmd.clone, body=%wide.region_27.29_spmd.clone.sunk | while | flops 100925448 | bytes 2754729 | solution.py:150
  615.2 43.8 %while.212 = (s32[]{:T(128)}, f32[2,256,128]{2,1,0:T(8,128)S(1)}, f32[2,64,2,128]{3,1,0,2:T(8,128)}, f32[2,64,2,128]{3,1,0,2:T(8,128)}, f32[2,64,2,256]{3,1,0,2:...) while((s32[]{:T(128)}, f32[2,256,128]{2,1,0:T(8,128)S(1)}, ...), condition=%wide.region_33.38_spmd.clone, body=%wide.region_32.37_spmd.clone.sunk | while | flops 485101568 | bytes 11272125 | solution.py:101
  673.0 12.7 collective-permute-done.2
  690.9 33.6 %all-reduce.40.cloned.1.call-done = f32[128,1024]{1,0:T(8,128)} async-done(((f32[128,1024]{1,0:T(8,128)}), f32[128,1024]{1,0:T(8,128)}) %all-reduce.40.cloned.1.call-update) | async-done | bytes 524304 | tf_op jit(solution)/shard_map/psum | solution.py:310
  731.5 33.5 %all-reduce.42.cloned.1.call-done = f32[128,1024]{1,0:T(8,128)} async-done(((f32[128,1024]{1,0:T(8,128)}), f32[128,1024]{1,0:T(8,128)}) %all-reduce.42.cloned.1.call-update) | async-done | bytes 524304 | tf_op jit(solution)/shard_map/psum | solution.py:278
  775.5 33.5 %while.215 = (s32[]{:T(128)}, f32[2,256,128]{2,1,0:T(8,128)S(1)}, f32[2,2,64,64]{3,2,1,0:T(8,128)S(1)}, f32[2,64,2,1]{1,2,3,0:T(2,128)S(1)}, f32[2,64,2,1]{1,2,3...) while((s32[]{:T(128)}, f32[2,256,128]{2,1,0:T(8,128)S(1)}, ...), condition=%wide.region_45.50_spmd.clone.clone, body=%wide.region_43.49_spmd.clone.clone.sunk | while | flops 164024704 | bytes 3990809 | solution.py:101
  809.0 14.1 all-gather.17.cloned.1.call-done
  823.1 19.6 %while.219 = (s32[]{:T(128)}, f32[2,256,128]{1,2,0:T(8,128)S(1)}, s32[]{:T(128)}, f32[8,2,128,128]{3,2,1,0:T(8,128)}, f32[8,2,256,128]{3,2,1,0:T(8,128)}, /*index=5*/s32[]{:T(128)}, s32[]{:T(128)}, s32[]{:T(128)}, s32[]{:T(128)}) while((s32[]{:T(128)}, f32[2,256,128]{1,2,0:T(8,128)S(1)}, s32[]{:T(128)}, ...), condition=%wide.region_42.47_spmd.clone, body=%wide.region_41.46_spmd.clone.sunk | while | flops 100925448 | bytes 2754729 | solution.py:150
  843.7 35.4 %while.213 = (s32[]{:T(128)}, f32[2,256,128]{2,1,0:T(8,128)S(1)}, f32[2,64,2,128]{3,1,0,2:T(8,128)S(1)}, f32[2,64,2,128]{3,1,0,2:T(8,128)S(1)}, f32[2,64,2,256]{...) while((s32[]{:T(128)}, f32[2,256,128]{2,1,0:T(8,128)S(1)}, ...), condition=%wide.region_47.52_spmd.clone, body=%wide.region_46.51_spmd.clone.sunk | while | flops 485101568 | bytes 8618345 | solution.py:101
  886.8 11.9 collective-permute-done.3
  945.9 38.6 %all-reduce.31 = (f32[2,1024]{1,0:T(2,128)}, f32[2,4,1024]{2,1,0:T(4,128)}, f32[2,256]{1,0:T(2,128)}, f32[2,1024]{1,0:T(2,128)}) all-reduce(f32[2,1024]{1,0:T(2,128)S(1)} %pad_maximum_fusion.8, f32[2,4,1024]{2,1,0:T(4,128)S(1)} %pad_maximum_fusion.7, ...), channel_id=1, replica_groups=mesh['seq'=8,'head'=4] {'seq'}, use_global_device_ids=true, to_apply=%region_54.59 | all-reduce | flops 12800 | bytes 102400 | tf_op jit(solution)/shard_map/psum | solution.py:394
  986.5 46.7 %reduce-scatter.20.cloned.1.call-done = f32[2,512,128]{2,1,0:T(8,128)} async-done(((f32[2,512,1024]{2,1,0:T(8,128)}), f32[2,512,128]{2,1,0:T(8,128)}) %reduce-scatter.20.cloned.1.call-update) | async-done | bytes 524304 | tf_op jit(solution)/shard_map/reduce_scatter | solution.py:383
  1033.2 114.8 %reduce-scatter.26.cloned.1.call-done = f32[2,704,128]{2,1,0:T(8,128)} async-done(((f32[2,704,1024]{2,1,0:T(8,128)}), f32[2,704,128]{2,1,0:T(8,128)}) %reduce-scatter.26.cloned.1.call-update) | async-done | bytes 720912 | tf_op jit(solution)/shard_map/reduce_scatter | solution.py:386
  1148.0 114.5 %reduce-scatter.22.cloned.1.call-done = f32[2,128,704]{1,2,0:T(8,128)} async-done(((f32[2,1024,704]{1,2,0:T(8,128)}), f32[2,128,704]{1,2,0:T(8,128)}) %reduce-scatter.22.cloned.1.call-update) | async-done | bytes 720912 | tf_op jit(solution)/shard_map/reduce_scatter | solution.py:384
  1262.5 114.5 %reduce-scatter.24.cloned.1.call-done = f32[2,128,704]{1,2,0:T(8,128)} async-done(((f32[2,1024,704]{1,2,0:T(8,128)}), f32[2,128,704]{1,2,0:T(8,128)}) %reduce-scatter.24.cloned.1.call-update) | async-done | bytes 720912 | tf_op jit(solution)/shard_map/reduce_scatter | solution.py:385
  1377.0 211.0 %reduce-scatter.18.cloned.1.call-done = f32[2,128,1536]{2,1,0:T(8,128)} async-done(((f32[2,1024,1536]{2,1,0:T(8,128)}), f32[2,128,1536]{2,1,0:T(8,128)}) %reduce-scatter.18.cloned.1.call-update) | async-done | bytes 1572880 | tf_op jit(solution)/shard_map/reduce_scatter | solution.py:382
  (1071 shorter events, 518.6 us)
Async XLA Ops:
  7.2 105.8 %all-gather.7.cloned.1.call-start = ((), (), s32[]{:S(2)}) async-start(), calls=%async_computation.9 | async-start | bytes 1179648 | tf_op jit(solution)/shard_map/all_gather | solution.py:117
  9.1 239.5 %copy-start.80 = (f32[1,1024]{1,0:T(1,128)}, f32[1,1024]{1,0:T(1,128)S(1)}, u32[]{:S(2)}) copy-start(f32[1,1024]{1,0:T(1,128)S(1)} %get-tuple-element.3506) | copy-start | bytes 12292
  20.6 16.1 %collective-permute-start = (f32[3,1024]{0,1:T(8,128)S(1)}, f32[3,1024]{0,1:T(8,128)S(1)}, u32[]{:S(2)}, u32[]{:S(2)}) collective-permute-start(f32[3,1024]{0,1:T(8,128)S(1)} %copy.512), channel_id=1, source_target_pairs={{0,4},{4,8},{8,12},{12,16},{16,20},{20,24},{24,28},{1,5},{5,9},{9,... | collective-permute-start | bytes 36872 | tf_op jit(solution)/shard_map/ppermute | solution.py:20
  25.7 243.9 %copy-start.102 = (f32[1,1,1024]{2,1,0:T(1,128)}, f32[1,1,1024]{2,1,0:T(1,128)S(1)}, u32[]{:S(2)}) copy-start(f32[1,1,1024]{2,1,0:T(1,128)S(1)} %get-tuple-element.3494) | copy-start | bytes 12292
  25.7 243.9 %copy-start.104 = (f32[1,1,1024]{2,1,0:T(1,128)}, f32[1,1,1024]{2,1,0:T(1,128)S(1)}, u32[]{:S(2)}) copy-start(f32[1,1,1024]{2,1,0:T(1,128)S(1)} %get-tuple-element.3495) | copy-start | bytes 12292
  25.7 243.9 %copy-start.106 = (f32[1,1,1024]{2,1,0:T(1,128)}, f32[1,1,1024]{2,1,0:T(1,128)S(1)}, u32[]{:S(2)}) copy-start(f32[1,1,1024]{2,1,0:T(1,128)S(1)} %get-tuple-element.3496) | copy-start | bytes 12292
  25.8 243.9 %copy-start.108 = (f32[1,1,1024]{2,1,0:T(1,128)}, f32[1,1,1024]{2,1,0:T(1,128)S(1)}, u32[]{:S(2)}) copy-start(f32[1,1,1024]{2,1,0:T(1,128)S(1)} %get-tuple-element.3497) | copy-start | bytes 12292
  69.6 114.1 %copy-start.57 = (f32[2,64,2,384]{3,1,0,2:T(8,128)}, f32[2,64,2,384]{3,1,0,2:T(8,128)S(1)}, u32[]{:S(2)}) copy-start(f32[2,64,2,384]{3,1,0,2:T(8,128)S(1)} %get-tuple-element.2055) | copy-start | bytes 1179652
  70.4 93.2 %all-gather.9.cloned.1.call-start = ((), (), s32[]{:S(2)}) async-start(), calls=%async_computation.10 | async-start | bytes 2359296 | tf_op jit(solution)/shard_map/all_gather | solution.py:118
  71.1 136.0 %reduce-scatter.10.cloned.1.call-start = ((), (), s32[]{:S(2)}) async-start(), calls=%async_computation.11 | async-start | bytes 655360 | tf_op jit(solution)/shard_map/reduce_scatter | solution.py:155
  71.2 348.6 %copy-start.122 = (f32[1,256]{1,0:T(1,128)}, f32[1,256]{1,0:T(1,128)S(1)}, u32[]{:S(2)}) copy-start(f32[1,256]{1,0:T(1,128)S(1)} %get-tuple-element.3508) | copy-start | bytes 3076
  186.9 54.5 %reduce-scatter.12.cloned.1.call-start = ((), (), s32[]{:S(2)}) async-start(), calls=%async_computation.12 | async-start | bytes 655360 | tf_op jit(solution)/shard_map/reduce_scatter | solution.py:155
  187.0 264.0 %copy-start.92 = (f32[1,1024]{1,0:T(1,128)}, f32[1,1024]{1,0:T(1,128)S(1)}, u32[]{:S(2)}) copy-start(f32[1,1024]{1,0:T(1,128)S(1)} %get-tuple-element.3504) | copy-start | bytes 12292
  219.1 129.8 %all-gather.11.cloned.1.call-start = ((), (), s32[]{:S(2)}) async-start(), calls=%async_computation.13 | async-start | bytes 1179648 | tf_op jit(solution)/shard_map/all_gather | solution.py:117
  248.6 477.8 %copy-start = (f32[128,1024]{1,0:T(8,128)}, f32[128,1024]{1,0:T(8,128)S(1)}, u32[]{:S(2)}) copy-start(f32[128,1024]{1,0:T(8,128)S(1)} %get-tuple-element.3414) | copy-start | bytes 1572868
  254.3 15.4 collective-permute-start.1
  306.9 92.4 %all-gather.13.cloned.1.call-start = ((), (), s32[]{:S(2)}) async-start(), calls=%async_computation.14 | async-start | bytes 2359296 | tf_op jit(solution)/shard_map/all_gather | solution.py:118
  307.7 136.2 %reduce-scatter.14.cloned.1.call-start = ((), (), s32[]{:S(2)}) async-start(), calls=%async_computation.15 | async-start | bytes 655360 | tf_op jit(solution)/shard_map/reduce_scatter | solution.py:155
  423.6 67.0 %all-reduce.38.cloned.1.call-start = ((), (), s32[]{:S(2)}) async-start(), calls=%async_computation.17 | async-start | bytes 1048576 | tf_op jit(solution)/shard_map/psum | solution.py:278
  456.5 58.9 %reduce-scatter.16.cloned.1.call-start = ((), (), s32[]{:S(2)}) async-start(), calls=%async_computation.16 | async-start | bytes 655360 | tf_op jit(solution)/shard_map/reduce_scatter | solution.py:155
  459.2 120.6 %all-gather.15.cloned.1.call-start = ((), (), s32[]{:S(2)}) async-start(), calls=%async_computation.18 | async-start | bytes 2359296 | tf_op jit(solution)/shard_map/all_gather | solution.py:137
  529.6 194.8 %all-reduce.40.cloned.1.call-start = ((), (), s32[]{:S(2)}) async-start(), calls=%async_computation.19 | async-start | bytes 1048576 | tf_op jit(solution)/shard_map/psum | solution.py:310
  671.4 14.3 collective-permute-start.2
  690.8 74.1 %all-reduce.42.cloned.1.call-start = ((), (), s32[]{:S(2)}) async-start(), calls=%async_computation.20 | async-start | bytes 1048576 | tf_op jit(solution)/shard_map/psum | solution.py:278
  731.3 91.8 %all-gather.17.cloned.1.call-start = ((), (), s32[]{:S(2)}) async-start(), calls=%async_computation.21 | async-start | bytes 2359296 | tf_op jit(solution)/shard_map/all_gather | solution.py:137
  773.3 171.3 %all-reduce.44.cloned.1.call-start = ((), (), s32[]{:S(2)}) async-start(), calls=%async_computation.22 | async-start | bytes 1048576 | tf_op jit(solution)/shard_map/psum | solution.py:310
  884.7 14.0 collective-permute-start.3
  904.8 128.5 %reduce-scatter.20.cloned.1.call-start = ((), (), s32[]{:S(2)}) async-start(), calls=%async_computation.24 | async-start | bytes 4718592 | tf_op jit(solution)/shard_map/reduce_scatter | solution.py:383
  907.6 240.4 %reduce-scatter.26.cloned.1.call-start = ((), (), s32[]{:S(2)}) async-start(), calls=%async_computation.27 | async-start | bytes 6488064 | tf_op jit(solution)/shard_map/reduce_scatter | solution.py:386
  912.7 349.8 %reduce-scatter.22.cloned.1.call-start = ((), (), s32[]{:S(2)}) async-start(), calls=%async_computation.25 | async-start | bytes 6488064 | tf_op jit(solution)/shard_map/reduce_scatter | solution.py:384
  917.8 459.2 %reduce-scatter.24.cloned.1.call-start = ((), (), s32[]{:S(2)}) async-start(), calls=%async_computation.26 | async-start | bytes 6488064 | tf_op jit(solution)/shard_map/reduce_scatter | solution.py:385
  922.8 665.1 %reduce-scatter.18.cloned.1.call-start = ((), (), s32[]{:S(2)}) async-start(), calls=%async_computation.23 | async-start | bytes 14155776 | tf_op jit(solution)/shard_map/reduce_scatter | solution.py:382
  (180 other events, 2248.9 us)
Sparse Core Ops, SparseCore 0:
  70.5 42.4 all-gather.6
  115.7 47.7 all-gather.8
  187.0 20.1 reduce-scatter.9
  219.2 22.1 reduce-scatter.11
  307.1 41.8 all-gather.10
  351.5 47.7 all-gather.12
  423.7 20.1 reduce-scatter.13
  456.6 33.9 all-reduce.37
  493.7 21.7 reduce-scatter.15
  529.8 50.0 all-gather.14
  690.9 33.4 all-reduce.39
  731.4 33.4 all-reduce.41
  773.4 49.6 all-gather.16
  904.9 34.1 all-reduce.43
  943.2 90.0 reduce-scatter.19
  1037.3 110.6 reduce-scatter.25
  1152.1 110.3 reduce-scatter.21
  1266.6 110.3 reduce-scatter.23
  1381.2 206.7 reduce-scatter.17
where the time goes:
time: 1610 us; the launch traced here: 1590 us
  waiting for transfers between devices  1020 us (63%)
  other arithmetic  197 us (12%)
  matrix products  162 us (10%)
  local copies, waits for them, and re-layouts  107 us (7%)
  blocking collectives  72.1 us (4%)
  between operations  16.9 us (1%)
    reduce_scatter x1, waiting for transfers between devices, body(): lax.psum_scatter(large_stack[0], 'seq', scatter_dimension=1, tiled=True)  211 us
    another operation x32, other arithmetic, span_step(): lax.linalg.triangular_solve(system, right_side, left_side=True, lower=True)  122 us
    reduce_scatter x1, waiting for transfers between devices, body(): lax.psum_scatter(large_stack[4], 'seq', scatter_dimension=2, tiled=True)  115 us
    reduce_scatter x1, waiting for transfers between devices, body(): lax.psum_scatter(large_stack[3], 'seq', scatter_dimension=1, tiled=True)  115 us
    reduce_scatter x1, waiting for transfers between devices, body(): lax.psum_scatter(large_stack[2], 'seq', scatter_dimension=1, tiled=True)  114 us
    all_gather x2, waiting for transfers between devices, state_prefix(): lax.all_gather(offset, 'seq', axis=0, tiled=True)  101 us
    all_gather x2, waiting for transfers between devices, state_prefix(): lax.all_gather(transfer, 'seq', axis=0, tiled=True)  82.9 us
    reduce_scatter x4, waiting for transfers between devices, head_total(): lax.psum_scatter(partial_sum, 'head', scatter_dimension=1, tiled=True)  78.4 us
  transfers between devices with their start and end apart: 23, of which 22 were waited for; matrix products, arithmetic and copies ran while one was open for 8% of the time, Pallas kernels for 0%

commit v1 on v0

--- a/solution.py
+++ b/solution.py
@@ -1,3 +1,4 @@
+import functools
 import jax
 import jax.numpy as jnp
 from jax import lax
@@ -12,6 +13,35 @@
 norm_eps = 1e-06
 gate_unit = 1.0 / 1048576.0
 beta_unit = 1.0 / 1024.0
+
+
+def change_files(in_array, axis_name):
+    f_now, t_next, newest = (lax.axis_size(axis_name), lax.axis_index(axis_name), in_array.shape[0])
+    block_next = lax.dynamic_update_slice_in_dim(
+        jnp.zeros(
+            [ii * f_now if w == 0 else ii for w, ii in enumerate(in_array.shape)], in_array.dtype
+        ),
+        in_array,
+        t_next * newest,
+        axis=0,
+    )
+    back = w_next = in_array
+    no = 1
+    while no < f_now // 2 + 1:
+        back = lax.ppermute(back, axis_name, [(w, (w + 1) % f_now) for w in range(f_now)])
+        block_next = lax.dynamic_update_slice_in_dim(
+            block_next, back, (t_next - no) % f_now * newest, axis=0
+        )
+        if 2 * no < f_now:
+            w_next = lax.ppermute(w_next, axis_name, [(w, (w - 1) % f_now) for w in range(f_now)])
+            block_next = lax.dynamic_update_slice_in_dim(
+                block_next, w_next, (t_next + no) % f_now * newest, axis=0
+            )
+        no += 1
+    return block_next
+
+
+meet_steps_all = functools.partial(change_files, axis_name="seq")
 
 
 def from_behind(array, axis, by):
@@ -115,7 +145,7 @@
 def state_prefix(transfer, offset):
     all_transfer, all_offset = (
         lax.all_gather(transfer, "seq", axis=0, tiled=True),
-        lax.all_gather(offset, "seq", axis=0, tiled=True),
+        meet_steps_all(offset),
     )
     devices = lax.axis_size("seq")
     position = lax.axis_index("seq")

time: 1610 us -> 1560 us (0.969)
  waiting for transfers between devices: 1020 us -> 875 us
  starting transfers between devices: 13.3 us -> 55 us
  local copies, waits for them, and re-layouts: 107 us -> 148 us
    all_gather x2 -> x0, waiting for transfers between devices: 101 us -> none  [state_prefix(): lax.all_gather(offset, 'seq', axis=0, tiled=True)]
    all_gather x2, waiting for transfers between devices: 82.9 us -> 0.01 us  [state_prefix(): lax.all_gather(transfer, 'seq', axis=0, tiled=True)]
    ppermute x0 -> x14, waiting for transfers between devices: none -> 54 us  [the longest x8 44.6 us: change_files(): lax.ppermute(back, axis_name, [(w, (w + 1) % f_now) for w in range(f_now)])]
    ppermute x0 -> x14, starting transfers between devices: none -> 41.9 us  [the longest x6 27.3 us: change_files(): lax.ppermute(w_next, axis_name, [(w, (w - 1) % f_now) for w in range(f_no...]
    dynamic_slice x32 -> x0, local copies, waits for them, and re-layouts: 17.7 us -> none  [advance(): offsets_all[index_now]]
  transfers between devices with their start and end apart: 23 -> 35, of which waited for: 22 -> 29; matrix products, arithmetic and copies ran while one was open for 8% -> 11% of each run, Pallas kernels for 0% -> 0%
where the time goes in v1:
time: 1560 us; the launch traced here: 1540 us
  waiting for transfers between devices  875 us (56%)
  other arithmetic  209 us (13%)
  matrix products  167 us (11%)
  local copies, waits for them, and re-layouts  148 us (9%)
  blocking collectives  72.2 us (5%)
  starting transfers between devices  55 us (4%)
  between operations  16.6 us (1%)
    reduce_scatter x1, waiting for transfers between devices, body(): lax.psum_scatter(large_stack[0], 'seq', scatter_dimension=1, tiled=True)  211 us
    another operation x32, other arithmetic, span_step(): lax.linalg.triangular_solve(system, right_side, left_side=True, lower=True)  122 us
    reduce_scatter x1, waiting for transfers between devices, body(): lax.psum_scatter(large_stack[4], 'seq', scatter_dimension=2, tiled=True)  115 us
    reduce_scatter x1, waiting for transfers between devices, body(): lax.psum_scatter(large_stack[3], 'seq', scatter_dimension=1, tiled=True)  115 us
    reduce_scatter x1, waiting for transfers between devices, body(): lax.psum_scatter(large_stack[2], 'seq', scatter_dimension=1, tiled=True)  114 us
    reduce_scatter x4, waiting for transfers between devices, head_total(): lax.psum_scatter(partial_sum, 'head', scatter_dimension=1, tiled=True)  77.9 us
    psum x2, waiting for transfers between devices, layer_backward(): grad_normed_two = lax.psum(ffn_partial, 'head')  61.7 us
    reduce_scatter x1, waiting for transfers between devices, body(): lax.psum_scatter(large_stack[1], 'seq', scatter_dimension=2, tiled=True)  46.8 us
  transfers between devices with their start and end apart: 35, of which 29 were waited for; matrix products, arithmetic and copies ran while one was open for 11% of the time, Pallas kernels for 0%

profile of v1, /device:TPU:0, one launch (start us, length us, event | category | flops | bytes accessed | tf_op | source)
XLA Modules:
  0.0 1544.8 jit_solution(12813251816766755993)
XLA Ops:
  41.0 29.7 %while.210 = (s32[]{:T(128)}, f32[2,384,128]{2,1,0:T(8,128)S(1)}, f32[2,64,2,384]{3,1,0,2:T(8,128)S(1)}, f32[2,64,2]{1,2,0:T(2,128)}, f32[2,64,2]{1,2,0:T(2,128)...) while((s32[]{:T(128)}, f32[2,384,128]{2,1,0:T(8,128)S(1)}, ...), condition=%wide.region_5.7_spmd, body=%wide.region_3.6_spmd.sunk | while | flops 340353152 | bytes 4627117 | solution.py:131
  42.6 9.8 custom-call.34
  57.5 9.8 custom-call.34
  107.4 11.1 collective-permute-done.5
  131.3 12.1 while.216
  146.8 20.1 %reduce-scatter.10.cloned.1.call-done = f32[128,256]{1,0:T(8,128)} async-done(((f32[128,1024]{1,0:T(8,128)}), f32[128,256]{1,0:T(8,128)}) %reduce-scatter.10.cloned.1.call-update) | async-done | bytes 131088 | tf_op jit(solution)/shard_map/reduce_scatter | solution.py:185
  184.0 17.5 %reduce-scatter.12.cloned.1.call-done = f32[128,256]{1,0:T(8,128)} async-done(((f32[128,1024]{1,0:T(8,128)}), f32[128,256]{1,0:T(8,128)}) %reduce-scatter.12.cloned.1.call-update) | async-done | bytes 131088 | tf_op jit(solution)/shard_map/reduce_scatter | solution.py:185
  239.2 33.0 %while.211 = (s32[]{:T(128)}, f32[2,384,128]{2,1,0:T(8,128)S(1)}, f32[2,64,2,384]{3,1,0,2:T(8,128)}, f32[2,64,2]{1,2,0:T(2,128)}, f32[2,64,2]{1,2,0:T(2,128)}, /...) while((s32[]{:T(128)}, f32[2,384,128]{2,1,0:T(8,128)S(1)}, ...), condition=%wide.region_17.19_spmd, body=%wide.region_15.18_spmd.sunk | while | flops 340353152 | bytes 4627117 | solution.py:131
  240.8 9.8 custom-call.35
  333.1 12.1 while.217
  354.4 17.3 %reduce-scatter.14.cloned.1.call-done = f32[128,256]{1,0:T(8,128)} async-done(((f32[128,1024]{1,0:T(8,128)}), f32[128,256]{1,0:T(8,128)}) %reduce-scatter.14.cloned.1.call-update) | async-done | bytes 131088 | tf_op jit(solution)/shard_map/reduce_scatter | solution.py:185
  389.5 28.2 %all-reduce.38.cloned.1.call-done = f32[128,1024]{1,0:T(8,128)} async-done(((f32[128,1024]{1,0:T(8,128)}), f32[128,1024]{1,0:T(8,128)}) %all-reduce.38.cloned.1.call-update) | async-done | bytes 524304 | tf_op jit(solution)/shard_map/psum | solution.py:308
  419.5 23.0 %reduce-scatter.16.cloned.1.call-done = f32[128,256]{1,0:T(8,128)} async-done(((f32[128,1024]{1,0:T(8,128)}), f32[128,256]{1,0:T(8,128)}) %reduce-scatter.16.cloned.1.call-update) | async-done | bytes 131088 | tf_op jit(solution)/shard_map/reduce_scatter | solution.py:185
  463.7 41.5 %while.214 = (s32[]{:T(128)}, f32[2,256,128]{2,1,0:T(8,128)S(1)}, f32[2,2,64,64]{3,2,1,0:T(8,128)}, f32[2,64,2,1]{1,2,3,0:T(2,128)}, f32[2,64,2,1]{1,2,3,0:T(2,1...) while((s32[]{:T(128)}, f32[2,256,128]{2,1,0:T(8,128)S(1)}, ...), condition=%wide.region_31.34_spmd.clone.clone, body=%wide.region_29.33_spmd.clone.clone.sunk | while | flops 164024704 | bytes 3922773 | solution.py:131
  471.0 9.9 custom-call.38
  506.0 32.4 %while.218 = (s32[]{:T(128)}, f32[2,256,128]{1,2,0:T(8,128)}, s32[]{:T(128)}, f32[8,2,128,128]{3,2,1,0:T(8,128)}, f32[8,2,256,128]{3,2,1,0:T(8,128)}, /*index=5*/s32[]{:T(128)}, s32[]{:T(128)}, s32[]{:T(128)}, s32[]{:T(128)}) while((s32[]{:T(128)}, f32[2,256,128]{1,2,0:T(8,128)}, s32[]{:T(128)}, f32[8,2,128,128]{3,2,1,0:T(8,128)}, ...), condition=%wide.region_28.30_spmd.clone, body=%wide.region_27.29_spmd.clone.sunk | while | flops 100925448 | bytes 2754729 | solution.py:180
  541.6 49.3 %while.212 = (s32[]{:T(128)}, f32[2,256,128]{2,1,0:T(8,128)S(1)}, f32[2,64,2,128]{3,1,0,2:T(8,128)}, f32[2,64,2,128]{3,1,0,2:T(8,128)}, f32[2,64,2,256]{3,1,0,2:...) while((s32[]{:T(128)}, f32[2,256,128]{2,1,0:T(8,128)S(1)}, ...), condition=%wide.region_33.38_spmd.clone, body=%wide.region_32.37_spmd.clone.sunk | while | flops 485101568 | bytes 12066977 | solution.py:131
  606.6 13.4 collective-permute-done.16
  624.5 34.0 %all-reduce.40.cloned.1.call-done = f32[128,1024]{1,0:T(8,128)} async-done(((f32[128,1024]{1,0:T(8,128)}), f32[128,1024]{1,0:T(8,128)}) %all-reduce.40.cloned.1.call-update) | async-done | bytes 524304 | tf_op jit(solution)/shard_map/psum | solution.py:340
  665.8 33.5 %all-reduce.42.cloned.1.call-done = f32[128,1024]{1,0:T(8,128)} async-done(((f32[128,1024]{1,0:T(8,128)}), f32[128,1024]{1,0:T(8,128)}) %all-reduce.42.cloned.1.call-update) | async-done | bytes 524304 | tf_op jit(solution)/shard_map/psum | solution.py:308
  714.4 39.3 %while.215 = (s32[]{:T(128)}, f32[2,256,128]{2,1,0:T(8,128)S(1)}, f32[2,2,64,64]{3,2,1,0:T(8,128)S(1)}, f32[2,64,2,1]{1,2,3,0:T(2,128)S(1)}, f32[2,64,2,1]{1,2,3...) while((s32[]{:T(128)}, f32[2,256,128]{2,1,0:T(8,128)S(1)}, ...), condition=%wide.region_45.50_spmd.clone.clone, body=%wide.region_43.49_spmd.clone.clone.sunk | while | flops 164024704 | bytes 3956617 | solution.py:131
  721.4 9.9 custom-call.39
  741.0 9.8 custom-call.39
  758.2 19.6 %while.219 = (s32[]{:T(128)}, f32[2,256,128]{1,2,0:T(8,128)S(1)}, s32[]{:T(128)}, f32[8,2,128,128]{3,2,1,0:T(8,128)}, f32[8,2,256,128]{3,2,1,0:T(8,128)}, /*index=5*/s32[]{:T(128)}, s32[]{:T(128)}, s32[]{:T(128)}, s32[]{:T(128)}) while((s32[]{:T(128)}, f32[2,256,128]{1,2,0:T(8,128)S(1)}, s32[]{:T(128)}, ...), condition=%wide.region_42.47_spmd.clone, body=%wide.region_41.46_spmd.clone.sunk | while | flops 100925448 | bytes 2754729 | solution.py:180
  779.4 44.9 %while.213 = (s32[]{:T(128)}, f32[2,256,128]{2,1,0:T(8,128)S(1)}, f32[2,64,2,128]{3,1,0,2:T(8,128)}, f32[2,64,2,128]{3,1,0,2:T(8,128)S(1)}, f32[2,64,2,256]{3,1,...) while((s32[]{:T(128)}, f32[2,256,128]{2,1,0:T(8,128)S(1)}, ...), condition=%wide.region_47.52_spmd.clone, body=%wide.region_46.51_spmd.clone.sunk | while | flops 485101568 | bytes 7307113 | solution.py:131
  836.8 12.0 collective-permute-done.17
  896.2 38.5 %all-reduce.31 = (f32[2,1024]{1,0:T(2,128)}, f32[2,4,1024]{2,1,0:T(4,128)}, f32[2,256]{1,0:T(2,128)}, f32[2,1024]{1,0:T(2,128)}) all-reduce(f32[2,1024]{1,0:T(2,128)S(1)} %pad_maximum_fusion.8, f32[2,4,1024]{2,1,0:T(4,128)S(1)} %pad_maximum_fusion.7, ...), channel_id=1, replica_groups=mesh['seq'=8,'head'=4] {'seq'}, use_global_device_ids=true, to_apply=%region_54.59 | all-reduce | flops 12800 | bytes 102400 | tf_op jit(solution)/shard_map/psum | solution.py:424
  936.7 46.8 %reduce-scatter.20.cloned.1.call-done = f32[2,512,128]{2,1,0:T(8,128)} async-done(((f32[2,512,1024]{2,1,0:T(8,128)}), f32[2,512,128]{2,1,0:T(8,128)}) %reduce-scatter.20.cloned.1.call-update) | async-done | bytes 524304 | tf_op jit(solution)/shard_map/reduce_scatter | solution.py:413
  983.5 114.8 %reduce-scatter.26.cloned.1.call-done = f32[2,704,128]{2,1,0:T(8,128)} async-done(((f32[2,704,1024]{2,1,0:T(8,128)}), f32[2,704,128]{2,1,0:T(8,128)}) %reduce-scatter.26.cloned.1.call-update) | async-done | bytes 720912 | tf_op jit(solution)/shard_map/reduce_scatter | solution.py:416
  1098.3 114.5 %reduce-scatter.22.cloned.1.call-done = f32[2,128,704]{1,2,0:T(8,128)} async-done(((f32[2,1024,704]{1,2,0:T(8,128)}), f32[2,128,704]{1,2,0:T(8,128)}) %reduce-scatter.22.cloned.1.call-update) | async-done | bytes 720912 | tf_op jit(solution)/shard_map/reduce_scatter | solution.py:414
  1212.8 114.5 %reduce-scatter.24.cloned.1.call-done = f32[2,128,704]{1,2,0:T(8,128)} async-done(((f32[2,1024,704]{1,2,0:T(8,128)}), f32[2,128,704]{1,2,0:T(8,128)}) %reduce-scatter.24.cloned.1.call-update) | async-done | bytes 720912 | tf_op jit(solution)/shard_map/reduce_scatter | solution.py:415
  1327.3 210.8 %reduce-scatter.18.cloned.1.call-done = f32[2,128,1536]{2,1,0:T(8,128)} async-done(((f32[2,1024,1536]{2,1,0:T(8,128)}), f32[2,128,1536]{2,1,0:T(8,128)}) %reduce-scatter.18.cloned.1.call-update) | async-done | bytes 1572880 | tf_op jit(solution)/shard_map/reduce_scatter | solution.py:412
  (1079 shorter events, 616.7 us)
Async XLA Ops:
  7.2 124.1 %all-gather.5.cloned.1.call-start = ((), (), s32[]{:S(2)}) async-start(), calls=%async_computation.9 | async-start | bytes 1179648 | tf_op jit(solution)/shard_map/all_gather | solution.py:147
  20.6 16.1 %collective-permute-start = (f32[3,1024]{0,1:T(8,128)S(1)}, f32[3,1024]{0,1:T(8,128)S(1)}, u32[]{:S(2)}, u32[]{:S(2)}) collective-permute-start(f32[3,1024]{0,1:T(8,128)S(1)} %copy.568), channel_id=1, source_target_pairs={{0,4},{4,8},{8,12},{12,16},{16,20},{20,24},{24,28},{1,5},{5,9},{9,... | collective-permute-start | bytes 36872 | tf_op jit(solution)/shard_map/ppermute | solution.py:50
  71.5 95.4 %reduce-scatter.10.cloned.1.call-start = ((), (), s32[]{:S(2)}) async-start(), calls=%async_computation.10 | async-start | bytes 655360 | tf_op jit(solution)/shard_map/reduce_scatter | solution.py:185
  77.1 13.1 collective-permute-start.1
  81.8 21.1 %collective-permute-start.4 = (f32[2,256,128]{2,1,0:T(8,128)S(1)}, f32[2,256,128]{2,1,0:T(8,128)S(1)}, u32[]{:S(2)}, u32[]{:S(2)}) collective-permute-start(f32[2,256,128]{2,1,0:T(8,128)S(1)} %collective-permute-done.2), channel_id=1, source_target_pairs={{0,28},{4,0},{8,4},{12,8},{16,12},{20,16},{24,20},{28,24},{1,29},{... | collective-permute-start | bytes 786440 | tf_op jit(solution)/shard_map/ppermute | solution.py:36
  100.0 18.5 %collective-permute-start.5 = (f32[2,256,128]{2,1,0:T(8,128)S(1)}, f32[2,256,128]{2,1,0:T(8,128)S(1)}, u32[]{:S(2)}, u32[]{:S(2)}) collective-permute-start(f32[2,256,128]{2,1,0:T(8,128)S(1)} %collective-permute-done.3), channel_id=1, source_target_pairs={{0,4},{4,8},{8,12},{12,16},{16,20},{20,24},{24,28},{28,0},{1,5},{5... | collective-permute-start | bytes 786440 | tf_op jit(solution)/shard_map/ppermute | solution.py:31
  102.9 21.2 %collective-permute-start.6 = (f32[2,256,128]{2,1,0:T(8,128)S(1)}, f32[2,256,128]{2,1,0:T(8,128)S(1)}, u32[]{:S(2)}, u32[]{:S(2)}) collective-permute-start(f32[2,256,128]{2,1,0:T(8,128)S(1)} %collective-permute-done.4), channel_id=1, source_target_pairs={{0,28},{4,0},{8,4},{12,8},{16,12},{20,16},{24,20},{28,24},{1,29},{... | collective-permute-start | bytes 786440 | tf_op jit(solution)/shard_map/ppermute | solution.py:36
  146.7 54.9 %reduce-scatter.12.cloned.1.call-start = ((), (), s32[]{:S(2)}) async-start(), calls=%async_computation.11 | async-start | bytes 655360 | tf_op jit(solution)/shard_map/reduce_scatter | solution.py:185
  179.2 153.9 %all-gather.7.cloned.1.call-start = ((), (), s32[]{:S(2)}) async-start(), calls=%async_computation.12 | async-start | bytes 1179648 | tf_op jit(solution)/shard_map/all_gather | solution.py:147
  213.3 15.4 collective-permute-start.8
  272.9 98.8 %reduce-scatter.14.cloned.1.call-start = ((), (), s32[]{:S(2)}) async-start(), calls=%async_computation.13 | async-start | bytes 655360 | tf_op jit(solution)/shard_map/reduce_scatter | solution.py:185
  273.0 14.8 collective-permute-start.9
  275.5 15.2 collective-permute-start.10
  287.7 12.7 collective-permute-start.11
  290.7 14.0 collective-permute-start.12
  300.4 17.8 %collective-permute-start.13 = (f32[2,256,128]{2,1,0:T(8,128)}, f32[2,256,128]{2,1,0:T(8,128)}, u32[]{:S(2)}, u32[]{:S(2)}) collective-permute-start(f32[2,256,128]{2,1,0:T(8,128)} %collective-permute-done.11), channel_id=1, source_target_pairs={{0,4},{4,8},{8,12},{12,16},{16,20},{20,24},{24,28},{28,0},{1,5},{5... | collective-permute-start | bytes 786440 | tf_op jit(solution)/shard_map/ppermute | solution.py:31
  304.7 19.9 %collective-permute-start.14 = (f32[2,256,128]{2,1,0:T(8,128)}, f32[2,256,128]{2,1,0:T(8,128)}, u32[]{:S(2)}, u32[]{:S(2)}) collective-permute-start(f32[2,256,128]{2,1,0:T(8,128)} %collective-permute-done.12), channel_id=1, source_target_pairs={{0,28},{4,0},{8,4},{12,8},{16,12},{20,16},{24,20},{28,24},{1,29},{... | collective-permute-start | bytes 786440 | tf_op jit(solution)/shard_map/ppermute | solution.py:36
  318.3 13.0 collective-permute-start.15
  351.5 66.2 %all-reduce.38.cloned.1.call-start = ((), (), s32[]{:S(2)}) async-start(), calls=%async_computation.15 | async-start | bytes 1048576 | tf_op jit(solution)/shard_map/psum | solution.py:308
  383.6 59.0 %reduce-scatter.16.cloned.1.call-start = ((), (), s32[]{:S(2)}) async-start(), calls=%async_computation.14 | async-start | bytes 655360 | tf_op jit(solution)/shard_map/reduce_scatter | solution.py:185
  386.3 119.8 %all-gather.9.cloned.1.call-start = ((), (), s32[]{:S(2)}) async-start(), calls=%async_computation.16 | async-start | bytes 2359296 | tf_op jit(solution)/shard_map/all_gather | solution.py:167
  455.9 202.5 %all-reduce.40.cloned.1.call-start = ((), (), s32[]{:S(2)}) async-start(), calls=%async_computation.17 | async-start | bytes 1048576 | tf_op jit(solution)/shard_map/psum | solution.py:340
  603.9 16.1 %collective-permute-start.16 = (f32[3,1024]{0,1:T(8,128)}, f32[3,1024]{0,1:T(8,128)S(1)}, u32[]{:S(2)}, u32[]{:S(2)}) collective-permute-start(f32[3,1024]{0,1:T(8,128)} %slice.407), channel_id=1, source_target_pairs={{4,0},{8,4},{12,8},{16,12},{20,16},{24,20},{28,24},{5,1},{9,5},{13... | collective-permute-start | bytes 36872 | tf_op jit(solution)/shard_map/ppermute | solution.py:50
  624.4 74.8 %all-reduce.42.cloned.1.call-start = ((), (), s32[]{:S(2)}) async-start(), calls=%async_computation.18 | async-start | bytes 1048576 | tf_op jit(solution)/shard_map/psum | solution.py:308
  665.6 92.6 %all-gather.11.cloned.1.call-start = ((), (), s32[]{:S(2)}) async-start(), calls=%async_computation.19 | async-start | bytes 2359296 | tf_op jit(solution)/shard_map/all_gather | solution.py:167
  708.6 186.3 %all-reduce.44.cloned.1.call-start = ((), (), s32[]{:S(2)}) async-start(), calls=%async_computation.20 | async-start | bytes 1048576 | tf_op jit(solution)/shard_map/psum | solution.py:340
  834.7 14.0 collective-permute-start.17
  855.0 128.5 %reduce-scatter.20.cloned.1.call-start = ((), (), s32[]{:S(2)}) async-start(), calls=%async_computation.22 | async-start | bytes 4718592 | tf_op jit(solution)/shard_map/reduce_scatter | solution.py:413
  857.8 240.5 %reduce-scatter.26.cloned.1.call-start = ((), (), s32[]{:S(2)}) async-start(), calls=%async_computation.25 | async-start | bytes 6488064 | tf_op jit(solution)/shard_map/reduce_scatter | solution.py:416
  862.9 349.9 %reduce-scatter.22.cloned.1.call-start = ((), (), s32[]{:S(2)}) async-start(), calls=%async_computation.23 | async-start | bytes 6488064 | tf_op jit(solution)/shard_map/reduce_scatter | solution.py:414
  868.0 459.3 %reduce-scatter.24.cloned.1.call-start = ((), (), s32[]{:S(2)}) async-start(), calls=%async_computation.24 | async-start | bytes 6488064 | tf_op jit(solution)/shard_map/reduce_scatter | solution.py:415
  873.1 665.0 %reduce-scatter.18.cloned.1.call-start = ((), (), s32[]{:S(2)}) async-start(), calls=%async_computation.21 | async-start | bytes 14155776 | tf_op jit(solution)/shard_map/reduce_scatter | solution.py:412
  (184 other events, 3564.9 us)
Sparse Core Ops, SparseCore 0:
  71.6 56.9 all-gather.4
  146.8 19.9 reduce-scatter.9
  179.3 22.1 reduce-scatter.11
  273.0 56.1 all-gather.6
  351.7 19.9 reduce-scatter.13
  383.7 33.9 all-reduce.37
  420.8 21.7 reduce-scatter.15
  456.0 49.9 all-gather.8
  624.5 33.8 all-reduce.39
  665.7 33.4 all-reduce.41
  708.7 49.4 all-gather.10
  855.1 34.0 all-reduce.43
  893.4 90.0 reduce-scatter.19
  987.6 110.6 reduce-scatter.25
  1102.4 110.3 reduce-scatter.21
  1216.9 110.3 reduce-scatter.23
  1331.3 206.7 reduce-scatter.17
